TPU v7x, 512 devices: a whole 4x4x16 slice. The times are simulated.
512 devices in a mesh: view: 32 (over x_lo, z), row: 16 (over x_hi, y, core).
Axes of the slice: x: 4 (x_hi: 2, x_lo: 2; x = x_hi * 2 + x_lo), y: 4, z: 16, core: 2. Of those that a mesh axis runs over, the one named last changes fastest.
Arguments:
- light_field: float32 [256, 64, 1920], P('view', 'row'), may hold values from -6 to 6
Outputs:
- refined_disparity: float32 [256, 64, 1920], P('view', 'row')
All inputs are finite; a program needn't handle non-finite values.
Results may differ from a plain program's by a relative error of at most 0.00002.
Values sent between devices are 32-bit elements; how exact they have to be, the bound alone decides.
A program may use at most 128 MiB of HBM per device.

v0:
```python
import functools
import math

import jax
import jax.numpy as jnp
from jax import lax
from jax.experimental import pallas as pl
from jax.experimental.pallas import tpu as pltpu
from jax.sharding import PartitionSpec as P

DAMPING = 0.1
FLOOR = 0.05
LANES = 128
LOG2E = 1.4426950408889634
RANGE_SCALE = math.sqrt(LOG2E / 2.0)
MESH = pl.DeviceIdType.MESH


def moved(value, offset):
    if offset == 0:
        return value
    width = value.shape[-1]
    return pltpu.roll(value, (-offset) % width, value.ndim - 1)


def tensor_terms(space, angle):
    terms = []
    for left, right in ((space, space), (space, angle), (angle, angle)):
        a, b, c = (x * y for x, y in zip(left, right))
        terms.append((a + c) + 2.0 * b)
    return terms


def five(m2, m1, c0, p1, p2):
    return (m2 + p2) + 4.0 * (m1 + p1) + 6.0 * c0


def disparity_confidence(ss, sa, aa):
    disparity = -sa / (ss + DAMPING)
    spread = aa - ss
    total = aa + ss
    confidence = (spread * spread + 4.0 * sa * sa) / (total * total + DAMPING)
    return disparity, confidence


def kernel(chunks, x_ref, xv_ref, out_ref, lum, pair, wide, horiz, mw, moved_ref, *sems):
    n_row = lax.axis_size("row")
    n_u = lax.axis_size("view") // 2
    d = lax.axis_index("view")
    r = lax.axis_index("row")
    u = d // 2
    h = lax.rem(d, 2)
    rows, _, width = x_ref.shape
    padded = width + 2 * LANES
    step = width // chunks
    inner = slice(LANES, LANES + width)

    up = u < n_u - 1
    down = u > 0
    both = jnp.logical_and(up, down)
    row_up = r < n_row - 1
    row_down = r > 0
    always = d >= 0
    held = (u >= 2, down, always, up, u < n_u - 2)
    to_up = {"view": d + 2}
    to_down = {"view": d - 2}
    to_pair = {"view": d + 1 - 2 * h}
    to_row_up = {"row": r + 1}
    to_row_down = {"row": r - 1}

    send_sems, recv_sems = sems
    used = [0]

    def copy(src, dst, device, sends, receives):
        i = used[0]
        used[0] += 1
        c = pltpu.make_async_remote_copy(
            src_ref=src, dst_ref=dst, send_sem=send_sems.at[i], recv_sem=recv_sems.at[i],
            device_id=device, device_id_type=MESH,
        )
        return c, sends, receives

    def start(item):
        pl.when(item[1])(item[0].start)

    def arrived(item):
        pl.when(item[2])(item[0].wait_recv)

    def left(item):
        pl.when(item[1])(item[0].wait_send)

    barrier = pltpu.get_barrier_semaphore()
    peers = ((up, to_up), (down, to_down), (always, to_pair), (row_up, to_row_up), (row_down, to_row_down))
    count = jnp.int32(0)
    for cond, device in peers:
        @pl.when(cond)
        def _(device=device):
            pl.semaphore_signal(barrier, inc=1, device_id=device, device_id_type=MESH)
        count = count + cond.astype(jnp.int32)
    pl.semaphore_wait(barrier, count)

    def cols(c):
        return pl.ds(LANES + c * step, step)

    near, far, edge, merged_edge = {}, {}, {}, {}
    all_copies = []
    pair_copy = copy(xv_ref.at[pl.ds(6 * (1 - h), 2)], pair, to_pair, always, always)
    all_copies.append(pair_copy)
    for c in range(chunks):
        own = x_ref.at[:, :, pl.ds(c * step, step)]
        near[c] = (
            copy(own, lum.at[1, pl.ds(3, rows), :, cols(c)], to_up, up, down),
            copy(own, lum.at[3, pl.ds(3, rows), :, cols(c)], to_down, down, up),
        )
        far[c] = (
            copy(lum.at[1, pl.ds(3, rows), :, cols(c)], lum.at[0, pl.ds(3, rows), :, cols(c)], to_up, both, held[0]),
            copy(lum.at[3, pl.ds(3, rows), :, cols(c)], lum.at[4, pl.ds(3, rows), :, cols(c)], to_down, both, held[4]),
        )
        all_copies += [*near[c], *far[c]]
        for k in range(5):
            if k == 2:
                high = x_ref.at[pl.ds(rows - 3, 3), :, pl.ds(c * step, step)]
                low = x_ref.at[pl.ds(0, 3), :, pl.ds(c * step, step)]
            else:
                high = lum.at[k, pl.ds(rows, 3), :, cols(c)]
                low = lum.at[k, pl.ds(3, 3), :, cols(c)]
            here = held[k]
            edge[c, k] = (
                copy(high, lum.at[k, pl.ds(0, 3), :, cols(c)], to_row_up,
                     jnp.logical_and(here, row_up), jnp.logical_and(here, row_down)),
                copy(low, lum.at[k, pl.ds(3 + rows, 3), :, cols(c)], to_row_down,
                     jnp.logical_and(here, row_down), jnp.logical_and(here, row_up)),
            )
            all_copies += [*edge[c, k]]
        merged_edge[c] = (
            copy(mw.at[:, pl.ds(rows, 3), :, cols(c)], mw.at[:, pl.ds(0, 3), :, cols(c)], to_row_up, row_up, row_down),
            copy(mw.at[:, pl.ds(3, 3), :, cols(c)], mw.at[:, pl.ds(3 + rows, 3), :, cols(c)], to_row_down, row_down, row_up),
        )
        all_copies += [*merged_edge[c]]

    start(pair_copy)
    for c in range(chunks):
        for item in near[c]:
            start(item)
    for c in range(chunks):
        for item in edge[c, 2]:
            start(item)

    zero_pad = jnp.zeros((8, LANES), jnp.float32)

    @pl.loop(0, rows + 6)
    def _(i):
        for side in (0, LANES + width):
            lum[2, i, :, side:side + LANES] = zero_pad
            for j in range(2):
                mw[j, i, :, side:side + LANES] = zero_pad

    for k in (0, 1, 3, 4):
        @pl.when(jnp.logical_not(held[k]))
        def _(k=k):
            @pl.loop(0, rows + 6)
            def _(i):
                lum[k, i] = jnp.zeros((8, padded), jnp.float32)

    for cond, first in ((jnp.logical_not(row_down), 0), (jnp.logical_not(row_up), 3 + rows)):
        @pl.when(cond)
        def _(first=first):
            for k in range(5):
                for i in range(first, first + 3):
                    lum[k, i] = jnp.zeros((8, padded), jnp.float32)
            for j in range(2):
                for i in range(first, first + 3):
                    mw[j, i] = jnp.zeros((8, padded), jnp.float32)

    for i in range(rows):
        lum[2, 3 + i, :, inner] = x_ref[i]
        wide[i, 8:16, inner] = x_ref[i]
        for side in (0, LANES + width):
            wide[i, :, side:side + LANES] = jnp.zeros((24, LANES), jnp.float32)
    arrived(pair_copy)
    for i in range(rows):
        for v in range(2):
            value = pair[v, i:i + 1, :]
            wide[i, 6 + v:7 + v, inner] = jnp.where(h == 1, value, 0.0)
            wide[i, 16 + v:17 + v, inner] = jnp.where(h == 0, value, 0.0)

    @pl.loop(0, rows)
    def _(i):
        views = [wide[i, 8 + o:16 + o, :] for o in (-2, -1, 0, 1, 2)]
        space = [moved(views[o], 1) - moved(views[o], -1) for o in (1, 2, 3)]
        angle = [views[o + 1] - views[o - 1] for o in (1, 2, 3)]
        ss, sa, aa = (
            five(*(moved(term, b) for b in (-2, -1, 0, 1, 2)))[:, inner] * (1.0 / 256.0)
            for term in tensor_terms(space, angle)
        )
        disparity, confidence = disparity_confidence(ss, sa, aa)
        horiz[0, i] = confidence * disparity
        horiz[1, i] = confidence

    for c in range(chunks):
        for item, k, on in ((near[c][0], 1, far[c][0]), (near[c][1], 3, far[c][1])):
            arrived(item)
            start(on)
            for e in edge[c, k]:
                start(e)

    for c in range(chunks):
        for e in edge[c, 2]:
            arrived(e)

    @pl.loop(0, rows + 6)
    def _(i):
        value = lum[2, i] * RANGE_SCALE
        for b in range(7):
            moved_ref[b, 0, i] = moved(value, b - 3)[:, inner]

    def vertical(c):
        @pl.loop(0, step // LANES)
        def _(t):
            out_at = pl.multiple_of(c * step + t * LANES, LANES)
            at = pl.multiple_of(out_at + LANES, LANES)
            terms = []
            for i in range(1, rows + 5):
                space = [lum[k, i + 1, :, pl.ds(at, LANES)] - lum[k, i - 1, :, pl.ds(at, LANES)] for k in (1, 2, 3)]
                angle = [lum[k + 1, i, :, pl.ds(at, LANES)] - lum[k - 1, i, :, pl.ds(at, LANES)] for k in (1, 2, 3)]
                terms.append(tensor_terms(space, angle))
            for i in range(rows):
                ss, sa, aa = (
                    five(*(terms[i + j][q] for j in range(5))) * (1.0 / 256.0) for q in range(3)
                )
                disparity, confidence = disparity_confidence(ss, sa, aa)
                product = horiz[0, i, :, pl.ds(out_at, LANES)]
                other = horiz[1, i, :, pl.ds(out_at, LANES)]
                total = other + confidence
                merged = (product + confidence * disparity) / (total + FLOOR)
                weight = FLOOR + 0.5 * total
                mw[0, 3 + i, :, pl.ds(at, LANES)] = merged * weight
                mw[1, 3 + i, :, pl.ds(at, LANES)] = weight

    for c in range(chunks):
        for item, k in ((far[c][0], 0), (far[c][1], 4)):
            arrived(item)
            for e in edge[c, k]:
                start(e)
        if c > 0:
            finish_chunk(c - 1, vertical, edge, merged_edge, arrived, start)
    finish_chunk(chunks - 1, vertical, edge, merged_edge, arrived, start)

    for c in range(chunks):
        for e in merged_edge[c]:
            arrived(e)

    @pl.loop(0, rows + 6)
    def _(i):
        for j in range(2):
            value = mw[j, i]
            for b in range(7):
                moved_ref[b, 1 + j, i] = moved(value, b - 3)[:, inner]

    @pl.loop(0, width // LANES)
    def _(t):
        at = pl.ds(pl.multiple_of(t * LANES, LANES), LANES)
        centre = [moved_ref[3, 0, 3 + i, :, at] for i in range(rows)]
        total = [None] * rows
        norm = [None] * rows
        for b in range(7):
            near_l = [moved_ref[b, 0, i, :, at] for i in range(rows + 6)]
            near_m = [moved_ref[b, 1, i, :, at] for i in range(rows + 6)]
            near_w = [moved_ref[b, 2, i, :, at] for i in range(rows + 6)]
            for i in range(rows):
                for a in range(7):
                    difference = near_l[i + a] - centre[i]
                    distance = ((a - 3) ** 2 + (b - 3) ** 2) / 8.0 * LOG2E
                    e = jnp.exp2(-distance - difference * difference)
                    m = e * near_m[i + a]
                    w = e * near_w[i + a]
                    total[i] = m if total[i] is None else total[i] + m
                    norm[i] = w if norm[i] is None else norm[i] + w
        for i in range(rows):
            out_ref[i, :, at] = total[i] / norm[i]

    for item in all_copies:
        left(item)


def finish_chunk(c, vertical, edge, merged_edge, arrived, start):
    for k in (0, 1, 3, 4):
        for e in edge[c, k]:
            arrived(e)
    vertical(c)
    for e in merged_edge[c]:
        start(e)


def local(light_field):
    views, rows, width = light_field.shape
    tiles = width // LANES
    chunks = 3 if tiles % 3 == 0 else 1
    padded = width + 2 * LANES
    copies = 1 + chunks * 16
    f32 = jnp.float32
    by_row = light_field.transpose(1, 0, 2)
    vmem = pl.BlockSpec(memory_space=pltpu.VMEM)
    refined = pl.pallas_call(
        functools.partial(kernel, chunks),
        out_shape=jax.ShapeDtypeStruct((rows, views, width), f32),
        in_specs=[vmem, vmem],
        out_specs=vmem,
        scratch_shapes=[
            pltpu.VMEM((5, rows + 6, views, padded), f32),
            pltpu.VMEM((2, rows, width), f32),
            pltpu.VMEM((rows, 24, padded), f32),
            pltpu.VMEM((2, rows, views, width), f32),
            pltpu.VMEM((2, rows + 6, views, padded), f32),
            pltpu.VMEM((7, 3, rows + 6, views, width), f32),
            pltpu.SemaphoreType.DMA((copies,)),
            pltpu.SemaphoreType.DMA((copies,)),
        ],
        compiler_params=pltpu.CompilerParams(
            collective_id=0, has_side_effects=True, vmem_limit_bytes=48 * 1024 * 1024
        ),
    )(by_row, light_field)
    return refined.transpose(1, 0, 2)


def solution(mesh):
    spec = P("view", "row", None)
    return jax.shard_map(local, mesh=mesh, in_specs=(spec,), out_specs=spec, check_vma=False)
```

profile of v0, /device:TPU:38, one launch (start us, length us, event | category | flops | bytes accessed | tf_op | source)
XLA Modules:
  0.0 60.7 jit_solution(4737200727092899844)
XLA Ops:
  0.0 0.0 copy-start
  0.0 1.0 %copy.5 = f32[8,4,1920]{2,0,1:T(8,128)S(1)} copy(f32[8,4,1920]{2,1,0:T(4,128)} %xv_ref.1) | data formatting | bytes 491520 | tf_op args[0]
  1.0 0.0 copy-done
  1.1 58.9 %shard_map.17 = f32[4,8,1920]{2,1,0:T(8,128)S(1)} custom-call(f32[4,8,1920]{2,1,0:T(8,128)S(1)} %bitcast.5, f32[8,4,1920]{2,1,0:T(4,128)S(1)} %copy-done), custom_call_target="tpu_custom_call" | custom-call | tf_op jit(solution)/shard_map/pallas_call | solution.py:304
  59.9 0.8 %copy.3 = f32[8,4,1920]{2,1,0:T(4,128)} copy(f32[8,4,1920]{2,0,1:T(8,128)S(1)} %bitcast.4) | data formatting | bytes 491520 | tf_op jit(solution)/shard_map/transpose | solution.py:323
Async XLA Ops:
  0.0 1.1 %copy-start = (f32[8,4,1920]{2,1,0:T(4,128)S(1)}, f32[8,4,1920]{2,1,0:T(4,128)}, u32[]{:S(2)}) copy-start(f32[8,4,1920]{2,1,0:T(4,128)} %xv_ref.1) | copy-start | bytes 737284
where the time goes:
time: 60.9 us; the launch traced here: 60.7 us
  Pallas kernels  58.9 us (97%)
  local copies, waits for them, and re-layouts  1.82 us (3%)
    pallas_call x1, Pallas kernels, local(): pl.pallas_call(functools.partial(kernel, chunks), out_shape=jax.ShapeDtyp...  58.9 us

commit v1 on v0

v1 whole, which is shorter than its diff:
```python
import functools
import math

import jax
import jax.numpy as jnp
from jax import lax
from jax.experimental import pallas as pl
from jax.experimental.pallas import tpu as pltpu
from jax.sharding import PartitionSpec as P

DAMPING = 0.1
FLOOR = 0.05
LANES = 128
LOG2E = 1.4426950408889634
RANGE_SCALE = math.sqrt(LOG2E / 2.0)
MESH = pl.DeviceIdType.MESH


def moved(value, offset):
    if offset == 0:
        return value
    width = value.shape[-1]
    return pltpu.roll(value, (-offset) % width, value.ndim - 1)


def tensor_terms(space, angle):
    terms = []
    for left, right in ((space, space), (space, angle), (angle, angle)):
        a, b, c = (x * y for x, y in zip(left, right))
        terms.append((a + c) + 2.0 * b)
    return terms


def five(m2, m1, c0, p1, p2):
    return (m2 + p2) + 4.0 * (m1 + p1) + 6.0 * c0


def disparity_confidence(ss, sa, aa):
    disparity = -sa / (ss + DAMPING)
    spread = aa - ss
    total = aa + ss
    confidence = (spread * spread + 4.0 * sa * sa) / (total * total + DAMPING)
    return disparity, confidence


def kernel(parts, x_ref, xv_ref, out_ref, lum, pair, wide, horiz, mw, moved_ref, sums, *sems):
    n_row = lax.axis_size("row")
    n_u = lax.axis_size("view") // 2
    d = lax.axis_index("view")
    r = lax.axis_index("row")
    u = d // 2
    h = lax.rem(d, 2)
    rows, _, width = x_ref.shape
    padded = width + 2 * LANES
    chunks = len(parts)
    begin = [LANES * sum(parts[:c]) for c in range(chunks)]
    inner = slice(LANES, LANES + width)

    up = u < n_u - 1
    down = u > 0
    both = jnp.logical_and(up, down)
    row_up = r < n_row - 1
    row_down = r > 0
    always = d >= 0
    held = (down, up, always, u >= 2, u < n_u - 2)
    to_up = {"view": d + 2}
    to_down = {"view": d - 2}
    to_pair = {"view": d + 1 - 2 * h}
    to_row_up = {"row": r + 1}
    to_row_down = {"row": r - 1}

    send_sems, recv_sems = sems
    used = [0]

    def copy(src, dst, device, sends, receives):
        i = used[0]
        used[0] += 1
        c = pltpu.make_async_remote_copy(
            src_ref=src, dst_ref=dst, send_sem=send_sems.at[i], recv_sem=recv_sems.at[i],
            device_id=device, device_id_type=MESH,
        )
        return c, sends, receives

    def start(item):
        pl.when(item[1])(item[0].start)

    def arrived(item):
        pl.when(item[2])(item[0].wait_recv)

    def left(item):
        pl.when(item[1])(item[0].wait_send)

    barrier = pltpu.get_barrier_semaphore()
    peers = ((up, to_up), (down, to_down), (always, to_pair), (row_up, to_row_up), (row_down, to_row_down))
    count = jnp.int32(0)
    for cond, device in peers:
        @pl.when(cond)
        def _(device=device):
            pl.semaphore_signal(barrier, inc=1, device_id=device, device_id_type=MESH)
        count = count + cond.astype(jnp.int32)
    pl.semaphore_wait(barrier, count)

    slots = (3, 0, 2, 1, 4)
    own_rows = pl.ds(3, rows)

    def cols(c):
        return pl.ds(LANES + begin[c], LANES * parts[c])

    def row_pair(high, high_to, low, low_to):
        return copy(high, high_to, to_row_up, row_up, row_down), copy(low, low_to, to_row_down, row_down, row_up)

    near, far, near_edge, far_edge, merged_edge = {}, {}, {}, {}, {}
    pair_copy = copy(xv_ref.at[pl.ds(6 * (1 - h), 2)], pair, to_pair, always, always)
    all_cols = pl.ds(LANES, width)
    own_edge = row_pair(
        x_ref.at[pl.ds(rows - 3, 3)], lum.at[2, pl.ds(0, 3), :, all_cols],
        x_ref.at[pl.ds(0, 3)], lum.at[2, pl.ds(3 + rows, 3), :, all_cols],
    )
    all_copies = [pair_copy, *own_edge]
    for c in range(chunks):
        own = x_ref.at[:, :, pl.ds(begin[c], LANES * parts[c])]
        near[c] = (
            copy(own, lum.at[0, own_rows, :, cols(c)], to_up, up, down),
            copy(own, lum.at[1, own_rows, :, cols(c)], to_down, down, up),
        )
        far[c] = (
            copy(lum.at[0, own_rows, :, cols(c)], lum.at[3, own_rows, :, cols(c)], to_up, both, held[3]),
            copy(lum.at[1, own_rows, :, cols(c)], lum.at[4, own_rows, :, cols(c)], to_down, both, held[4]),
        )
        for edges, first, depth in ((near_edge, 0, 3), (far_edge, 3, 2)):
            two = pl.ds(first, 2)
            edges[c] = row_pair(
                lum.at[two, pl.ds(3 + rows - depth, depth), :, cols(c)], lum.at[two, pl.ds(3 - depth, depth), :, cols(c)],
                lum.at[two, pl.ds(3, depth), :, cols(c)], lum.at[two, pl.ds(3 + rows, depth), :, cols(c)],
            )
        merged_edge[c] = row_pair(
            mw.at[:, pl.ds(rows, 3), :, cols(c)], mw.at[:, pl.ds(0, 3), :, cols(c)],
            mw.at[:, pl.ds(3, 3), :, cols(c)], mw.at[:, pl.ds(3 + rows, 3), :, cols(c)],
        )
        all_copies += [*near[c], *far[c], *near_edge[c], *far_edge[c], *merged_edge[c]]

    start(pair_copy)
    for c in range(chunks):
        for item in near[c]:
            start(item)
    for e in own_edge:
        start(e)

    zero_pad = jnp.zeros((8, LANES), jnp.float32)

    @pl.loop(0, rows + 6)
    def _(i):
        for side in (0, LANES + width):
            lum[2, i, :, side:side + LANES] = zero_pad
            for j in range(2):
                mw[j, i, :, side:side + LANES] = zero_pad

    for k in (0, 1, 3, 4):
        @pl.when(jnp.logical_not(held[k]))
        def _(k=k):
            @pl.loop(3, 3 + rows)
            def _(i):
                lum[k, i] = jnp.zeros((8, padded), jnp.float32)

    for cond, first in ((jnp.logical_not(row_down), 0), (jnp.logical_not(row_up), 3 + rows)):
        @pl.when(cond)
        def _(first=first):
            for k in range(5):
                for i in range(first, first + 3):
                    lum[k, i] = jnp.zeros((8, padded), jnp.float32)
            for j in range(2):
                for i in range(first, first + 3):
                    mw[j, i] = jnp.zeros((8, padded), jnp.float32)

    for i in range(rows):
        lum[2, 3 + i, :, inner] = x_ref[i]
        wide[i, 8:16, inner] = x_ref[i]
        for side in (0, LANES + width):
            wide[i, :, side:side + LANES] = jnp.zeros((24, LANES), jnp.float32)
    arrived(pair_copy)
    for i in range(rows):
        for v in range(2):
            value = pair[v, i:i + 1, :]
            wide[i, 6 + v:7 + v, inner] = jnp.where(h == 1, value, 0.0)
            wide[i, 16 + v:17 + v, inner] = jnp.where(h == 0, value, 0.0)

    @pl.loop(0, rows)
    def _(i):
        views = [wide[i, 8 + o:16 + o, :] for o in (-2, -1, 0, 1, 2)]
        space = [moved(views[o], 1) - moved(views[o], -1) for o in (1, 2, 3)]
        angle = [views[o + 1] - views[o - 1] for o in (1, 2, 3)]
        ss, sa, aa = (
            five(*(moved(term, b) for b in (-2, -1, 0, 1, 2)))[:, inner] * (1.0 / 256.0)
            for term in tensor_terms(space, angle)
        )
        disparity, confidence = disparity_confidence(ss, sa, aa)
        horiz[0, i] = confidence * disparity
        horiz[1, i] = confidence

    for c in range(chunks):
        for item, on in zip(near[c], far[c]):
            arrived(item)
            start(on)
        for e in near_edge[c]:
            start(e)

    for e in own_edge:
        arrived(e)

    @pl.loop(0, rows + 6)
    def _(i):
        value = lum[2, i] * RANGE_SCALE
        for b in range(7):
            moved_ref[b, 0, i] = moved(value, b - 3)[:, inner]

    def vertical(c):
        @pl.loop(0, parts[c])
        def _(t):
            out_at = pl.multiple_of(begin[c] + t * LANES, LANES)
            at = pl.multiple_of(out_at + LANES, LANES)
            terms = []
            for i in range(1, rows + 5):
                space = [lum[k, i + 1, :, pl.ds(at, LANES)] - lum[k, i - 1, :, pl.ds(at, LANES)] for k in slots[1:4]]
                views = [lum[k, i, :, pl.ds(at, LANES)] for k in slots]
                angle = [views[o + 1] - views[o - 1] for o in (1, 2, 3)]
                terms.append(tensor_terms(space, angle))
            for i in range(rows):
                ss, sa, aa = (
                    five(*(terms[i + j][q] for j in range(5))) * (1.0 / 256.0) for q in range(3)
                )
                disparity, confidence = disparity_confidence(ss, sa, aa)
                product = horiz[0, i, :, pl.ds(out_at, LANES)]
                other = horiz[1, i, :, pl.ds(out_at, LANES)]
                total = other + confidence
                merged = (product + confidence * disparity) / (total + FLOOR)
                weight = FLOOR + 0.5 * total
                mw[0, 3 + i, :, pl.ds(at, LANES)] = merged * weight
                mw[1, 3 + i, :, pl.ds(at, LANES)] = weight

    def merge(c):
        for e in (*near_edge[c], *far_edge[c]):
            arrived(e)
        vertical(c)
        for e in merged_edge[c]:
            start(e)

    def refine(c, own):
        if not own:
            for e in merged_edge[c]:
                arrived(e)
        first = max(sum(parts[:c]) - 1, 0)
        last = sum(parts) if c == chunks - 1 else sum(parts[:c + 1]) - 1
        span = (last - first) * LANES

        def shift(i):
            for j in range(2):
                value = mw[j, i, :, first * LANES:last * LANES + 2 * LANES]
                for b in range(7):
                    moved_ref[b, 1 + j, i, :, first * LANES:last * LANES] = moved(value, b - 3)[:, LANES:LANES + span]

        for start_row, stop_row in ((3, 3 + rows),) if own else ((0, 3), (3 + rows, 6 + rows)):
            pl.loop(start_row, stop_row)(shift)
        used_rows = [i for i in range(rows + 6) if (3 <= i < 3 + rows) == own]

        @pl.loop(first, last)
        def _(t):
            at = pl.ds(pl.multiple_of(t * LANES, LANES), LANES)
            centre = [moved_ref[3, 0, 3 + i, :, at] for i in range(rows)]
            total = [None if own else sums[0, i, :, at] for i in range(rows)]
            norm = [None if own else sums[1, i, :, at] for i in range(rows)]
            for b in range(7):
                near_l = {i: moved_ref[b, 0, i, :, at] for i in used_rows}
                near_m = {i: moved_ref[b, 1, i, :, at] for i in used_rows}
                near_w = {i: moved_ref[b, 2, i, :, at] for i in used_rows}
                for i in range(rows):
                    for a in range(7):
                        if i + a not in used_rows:
                            continue
                        difference = near_l[i + a] - centre[i]
                        distance = ((a - 3) ** 2 + (b - 3) ** 2) / 8.0 * LOG2E
                        e = jnp.exp2(-distance - difference * difference)
                        m = e * near_m[i + a]
                        w = e * near_w[i + a]
                        total[i] = m if total[i] is None else total[i] + m
                        norm[i] = w if norm[i] is None else norm[i] + w
            for i in range(rows):
                if own:
                    sums[0, i, :, at] = total[i]
                    sums[1, i, :, at] = norm[i]
                else:
                    out_ref[i, :, at] = total[i] / norm[i]

    for c in range(chunks + 2):
        if c < chunks:
            for item in far[c]:
                arrived(item)
            for e in far_edge[c]:
                start(e)
        if 1 <= c <= chunks:
            merge(c - 1)
            if c == chunks and c >= 2:
                refine(c - 2, False)
            refine(c - 1, True)
        if 2 <= c != chunks:
            refine(c - 2, False)

    for item in all_copies:
        left(item)


def local(light_field):
    views, rows, width = light_field.shape
    tiles = width // LANES
    parts = (tiles - 2 * tiles // 5, 2 * tiles // 5)
    padded = width + 2 * LANES
    copies = 3 + len(parts) * 10
    f32 = jnp.float32
    by_row = light_field.transpose(1, 0, 2)
    vmem = pl.BlockSpec(memory_space=pltpu.VMEM)
    refined = pl.pallas_call(
        functools.partial(kernel, parts),
        out_shape=jax.ShapeDtypeStruct((rows, views, width), f32),
        in_specs=[vmem, vmem],
        out_specs=vmem,
        scratch_shapes=[
            pltpu.VMEM((5, rows + 6, views, padded), f32),
            pltpu.VMEM((2, rows, width), f32),
            pltpu.VMEM((rows, 24, padded), f32),
            pltpu.VMEM((2, rows, views, width), f32),
            pltpu.VMEM((2, rows + 6, views, padded), f32),
            pltpu.VMEM((7, 3, rows + 6, views, width), f32),
            pltpu.VMEM((2, rows, views, width), f32),
            pltpu.SemaphoreType.DMA((copies,)),
            pltpu.SemaphoreType.DMA((copies,)),
        ],
        compiler_params=pltpu.CompilerParams(
            collective_id=0, has_side_effects=True, vmem_limit_bytes=48 * 1024 * 1024
        ),
    )(by_row, light_field)
    return refined.transpose(1, 0, 2)


def solution(mesh):
    spec = P("view", "row", None)
    return jax.shard_map(local, mesh=mesh, in_specs=(spec,), out_specs=spec, check_vma=False)
```

time: 60.9 us -> 55.5 us (0.911)
  Pallas kernels: 58.9 us -> 53.5 us
    pallas_call x1, Pallas kernels: 58.9 us -> 53.5 us  [local(): pl.pallas_call(functools.partial(kernel, parts), out_shape=jax.ShapeDtype...]
where the time goes in v1:
time: 55.5 us; the launch traced here: 55.3 us
  Pallas kernels  53.5 us (96%)
  local copies, waits for them, and re-layouts  1.82 us (3%)
    pallas_call x1, Pallas kernels, local(): pl.pallas_call(functools.partial(kernel, parts), out_shape=jax.ShapeDtype...  53.5 us

profile of v1, /device:TPU:38, one launch (start us, length us, event | category | flops | bytes accessed | tf_op | source)
XLA Modules:
  0.0 55.3 jit_solution(814646042149340780)
XLA Ops:
  0.0 0.0 copy-start
  0.0 1.0 %copy.5 = f32[8,4,1920]{2,0,1:T(8,128)S(1)} copy(f32[8,4,1920]{2,1,0:T(4,128)} %xv_ref.1) | data formatting | bytes 491520 | tf_op args[0]
  1.0 0.0 copy-done
  1.1 53.5 %shard_map.17 = f32[4,8,1920]{2,1,0:T(8,128)S(1)} custom-call(f32[4,8,1920]{2,1,0:T(8,128)S(1)} %bitcast.5, f32[8,4,1920]{2,1,0:T(4,128)S(1)} %copy-done), custom_call_target="tpu_custom_call" | custom-call | tf_op jit(solution)/shard_map/pallas_call | solution.py:320
  54.6 0.8 %copy.3 = f32[8,4,1920]{2,1,0:T(4,128)} copy(f32[8,4,1920]{2,0,1:T(8,128)S(1)} %bitcast.4) | data formatting | bytes 491520 | tf_op jit(solution)/shard_map/transpose | solution.py:340
Async XLA Ops:
  0.0 1.1 %copy-start = (f32[8,4,1920]{2,1,0:T(4,128)S(1)}, f32[8,4,1920]{2,1,0:T(4,128)}, u32[]{:S(2)}) copy-start(f32[8,4,1920]{2,1,0:T(4,128)} %xv_ref.1) | copy-start | bytes 737284

commit v2 on v1

--- a/solution.py
+++ b/solution.py
@@ -43,7 +43,7 @@
     return disparity, confidence
 
 
-def kernel(parts, x_ref, xv_ref, out_ref, lum, pair, wide, horiz, mw, moved_ref, sums, *sems):
+def kernel(parts, x_ref, xv_ref, out_ref, lum, pair, wide, horiz, mw, moved_ref, closeness, sums, *sems):
     n_row = lax.axis_size("row")
     n_u = lax.axis_size("view") // 2
     d = lax.axis_index("view")
@@ -212,6 +212,18 @@
         value = lum[2, i] * RANGE_SCALE
         for b in range(7):
             moved_ref[b, 0, i] = moved(value, b - 3)[:, inner]
+
+    @pl.loop(0, width // LANES)
+    def _(t):
+        at = pl.ds(pl.multiple_of(t * LANES, LANES), LANES)
+        centre = [moved_ref[3, 0, 3 + i, :, at] for i in range(rows)]
+        for b in range(7):
+            near_l = [moved_ref[b, 0, i, :, at] for i in range(rows + 6)]
+            for i in range(rows):
+                for a in range(7):
+                    difference = near_l[i + a] - centre[i]
+                    distance = ((a - 3) ** 2 + (b - 3) ** 2) / 8.0 * LOG2E
+                    closeness[7 * b + a, i, :, at] = jnp.exp2(-distance - difference * difference)
 
     def vertical(c):
         @pl.loop(0, parts[c])
@@ -265,20 +277,16 @@
         @pl.loop(first, last)
         def _(t):
             at = pl.ds(pl.multiple_of(t * LANES, LANES), LANES)
-            centre = [moved_ref[3, 0, 3 + i, :, at] for i in range(rows)]
             total = [None if own else sums[0, i, :, at] for i in range(rows)]
             norm = [None if own else sums[1, i, :, at] for i in range(rows)]
             for b in range(7):
-                near_l = {i: moved_ref[b, 0, i, :, at] for i in used_rows}
                 near_m = {i: moved_ref[b, 1, i, :, at] for i in used_rows}
                 near_w = {i: moved_ref[b, 2, i, :, at] for i in used_rows}
                 for i in range(rows):
                     for a in range(7):
                         if i + a not in used_rows:
                             continue
-                        difference = near_l[i + a] - centre[i]
-                        distance = ((a - 3) ** 2 + (b - 3) ** 2) / 8.0 * LOG2E
-                        e = jnp.exp2(-distance - difference * difference)
+                        e = closeness[7 * b + a, i, :, at]
                         m = e * near_m[i + a]
                         w = e * near_w[i + a]
                         total[i] = m if total[i] is None else total[i] + m
@@ -329,6 +337,7 @@
             pltpu.VMEM((2, rows, views, width), f32),
             pltpu.VMEM((2, rows + 6, views, padded), f32),
             pltpu.VMEM((7, 3, rows + 6, views, width), f32),
+            pltpu.VMEM((49, rows, views, width), f32),
             pltpu.VMEM((2, rows, views, width), f32),
             pltpu.SemaphoreType.DMA((copies,)),
             pltpu.SemaphoreType.DMA((copies,)),

time: 55.5 us -> 54.8 us (0.987)
  Pallas kernels: 53.5 us -> 52.8 us
    pallas_call x1, Pallas kernels: 53.5 us -> 52.8 us  [local(): pl.pallas_call(functools.partial(kernel, parts), out_shape=jax.ShapeDtype...]
where the time goes in v2:
time: 54.8 us; the launch traced here: 54.7 us
  Pallas kernels  52.8 us (96%)
  local copies, waits for them, and re-layouts  1.82 us (3%)
    pallas_call x1, Pallas kernels, local(): pl.pallas_call(functools.partial(kernel, parts), out_shape=jax.ShapeDtype...  52.8 us

profile of v2, /device:TPU:38, one launch (start us, length us, event | category | flops | bytes accessed | tf_op | source)
XLA Modules:
  0.0 54.7 jit_solution(4838754503902169832)
XLA Ops:
  0.0 0.0 copy-start
  0.0 1.0 %copy.5 = f32[8,4,1920]{2,0,1:T(8,128)S(1)} copy(f32[8,4,1920]{2,1,0:T(4,128)} %xv_ref.1) | data formatting | bytes 491520 | tf_op args[0]
  1.0 0.0 copy-done
  1.1 52.8 %shard_map.17 = f32[4,8,1920]{2,1,0:T(8,128)S(1)} custom-call(f32[4,8,1920]{2,1,0:T(8,128)S(1)} %bitcast.5, f32[8,4,1920]{2,1,0:T(4,128)S(1)} %copy-done), custom_call_target="tpu_custom_call" | custom-call | tf_op jit(solution)/shard_map/pallas_call | solution.py:328
  53.9 0.8 %copy.3 = f32[8,4,1920]{2,1,0:T(4,128)} copy(f32[8,4,1920]{2,0,1:T(8,128)S(1)} %bitcast.4) | data formatting | bytes 491520 | tf_op jit(solution)/shard_map/transpose | solution.py:349
Async XLA Ops:
  0.0 1.1 %copy-start = (f32[8,4,1920]{2,1,0:T(4,128)S(1)}, f32[8,4,1920]{2,1,0:T(4,128)}, u32[]{:S(2)}) copy-start(f32[8,4,1920]{2,1,0:T(4,128)} %xv_ref.1) | copy-start | bytes 737284

commit v3 on v2

--- a/solution.py
+++ b/solution.py
@@ -62,6 +62,10 @@
     row_up = r < n_row - 1
     row_down = r > 0
     always = d >= 0
+    low_half = r == n_row // 2 - 1
+    high_half = r == n_row // 2
+    middle = jnp.logical_or(low_half, high_half)
+    halo = jnp.where(high_half, 1, 3 + rows)
     held = (down, up, always, u >= 2, u < n_u - 2)
     to_up = {"view": d + 2}
     to_down = {"view": d - 2}
@@ -109,7 +113,15 @@
     def row_pair(high, high_to, low, low_to):
         return copy(high, high_to, to_row_up, row_up, row_down), copy(low, low_to, to_row_down, row_down, row_up)
 
-    near, far, near_edge, far_edge, merged_edge = {}, {}, {}, {}, {}
+    def apart(edges):
+        (high, high_sends, high_receives), (low, low_sends, low_receives) = edges
+        not_low, not_high = jnp.logical_not(low_half), jnp.logical_not(high_half)
+        return (
+            (high, jnp.logical_and(high_sends, not_low), jnp.logical_and(high_receives, not_high)),
+            (low, jnp.logical_and(low_sends, not_high), jnp.logical_and(low_receives, not_low)),
+        )
+
+    near, far, near_edge, far_edge, merged_edge, far_halo = {}, {}, {}, {}, {}, {}
     pair_copy = copy(xv_ref.at[pl.ds(6 * (1 - h), 2)], pair, to_pair, always, always)
     all_cols = pl.ds(LANES, width)
     own_edge = row_pair(
@@ -133,11 +145,19 @@
                 lum.at[two, pl.ds(3 + rows - depth, depth), :, cols(c)], lum.at[two, pl.ds(3 - depth, depth), :, cols(c)],
                 lum.at[two, pl.ds(3, depth), :, cols(c)], lum.at[two, pl.ds(3 + rows, depth), :, cols(c)],
             )
+        far_edge[c] = apart(far_edge[c])
+        beside = pl.ds(halo, 2)
+        far_halo[c] = (
+            copy(lum.at[0, beside, :, cols(c)], lum.at[3, beside, :, cols(c)], to_up,
+                 jnp.logical_and(both, middle), jnp.logical_and(held[3], middle)),
+            copy(lum.at[1, beside, :, cols(c)], lum.at[4, beside, :, cols(c)], to_down,
+                 jnp.logical_and(both, middle), jnp.logical_and(held[4], middle)),
+        )
         merged_edge[c] = row_pair(
             mw.at[:, pl.ds(rows, 3), :, cols(c)], mw.at[:, pl.ds(0, 3), :, cols(c)],
             mw.at[:, pl.ds(3, 3), :, cols(c)], mw.at[:, pl.ds(3 + rows, 3), :, cols(c)],
         )
-        all_copies += [*near[c], *far[c], *near_edge[c], *far_edge[c], *merged_edge[c]]
+        all_copies += [*near[c], *far[c], *near_edge[c], *far_edge[c], *far_halo[c], *merged_edge[c]]
 
     start(pair_copy)
     for c in range(chunks):
@@ -161,6 +181,12 @@
             @pl.loop(3, 3 + rows)
             def _(i):
                 lum[k, i] = jnp.zeros((8, padded), jnp.float32)
+
+    for k in (3, 4):
+        @pl.when(jnp.logical_and(jnp.logical_not(held[k]), middle))
+        def _(k=k):
+            for j in range(2):
+                lum[k, halo + j] = jnp.zeros((8, padded), jnp.float32)
 
     for cond, first in ((jnp.logical_not(row_down), 0), (jnp.logical_not(row_up), 3 + rows)):
         @pl.when(cond)
@@ -224,6 +250,12 @@
                     difference = near_l[i + a] - centre[i]
                     distance = ((a - 3) ** 2 + (b - 3) ** 2) / 8.0 * LOG2E
                     closeness[7 * b + a, i, :, at] = jnp.exp2(-distance - difference * difference)
+
+    for c in range(chunks):
+        pl.when(high_half)(near_edge[c][0][0].wait_recv)
+        pl.when(low_half)(near_edge[c][1][0].wait_recv)
+        for item in far_halo[c]:
+            start(item)
 
     def vertical(c):
         @pl.loop(0, parts[c])
@@ -250,7 +282,7 @@
                 mw[1, 3 + i, :, pl.ds(at, LANES)] = weight
 
     def merge(c):
-        for e in (*near_edge[c], *far_edge[c]):
+        for e in (*apart(near_edge[c]), *far_edge[c], *far_halo[c]):
             arrived(e)
         vertical(c)
         for e in merged_edge[c]:
@@ -321,7 +353,7 @@
     tiles = width // LANES
     parts = (tiles - 2 * tiles // 5, 2 * tiles // 5)
     padded = width + 2 * LANES
-    copies = 3 + len(parts) * 10
+    copies = 3 + len(parts) * 12
     f32 = jnp.float32
     by_row = light_field.transpose(1, 0, 2)
     vmem = pl.BlockSpec(memory_space=pltpu.VMEM)

time: 54.8 us -> 53 us (0.967)
  the two profiles are of different devices: /device:TPU:38 before, /device:TPU:6 now
where the time goes in v3:
time: 53 us; the launch traced here: 52.8 us
  Pallas kernels  51 us (96%)
  local copies, waits for them, and re-layouts  1.82 us (3%)
    pallas_call x1, Pallas kernels, local(): pl.pallas_call(functools.partial(kernel, parts), out_shape=jax.ShapeDtype...  51 us

profile of v3, /device:TPU:6, one launch (start us, length us, event | category | flops | bytes accessed | tf_op | source)
XLA Modules:
  0.0 52.8 jit_solution(562155671575988177)
XLA Ops:
  0.0 0.0 copy-start
  0.0 1.0 %copy.5 = f32[8,4,1920]{2,0,1:T(8,128)S(1)} copy(f32[8,4,1920]{2,1,0:T(4,128)} %xv_ref.1) | data formatting | bytes 491520 | tf_op args[0]
  1.0 0.0 copy-done
  1.1 51.0 %shard_map.17 = f32[4,8,1920]{2,1,0:T(8,128)S(1)} custom-call(f32[4,8,1920]{2,1,0:T(8,128)S(1)} %bitcast.5, f32[8,4,1920]{2,1,0:T(4,128)S(1)} %copy-done), custom_call_target="tpu_custom_call" | custom-call | tf_op jit(solution)/shard_map/pallas_call | solution.py:360
  52.1 0.8 %copy.3 = f32[8,4,1920]{2,1,0:T(4,128)} copy(f32[8,4,1920]{2,0,1:T(8,128)S(1)} %bitcast.4) | data formatting | bytes 491520 | tf_op jit(solution)/shard_map/transpose | solution.py:381
Async XLA Ops:
  0.0 1.1 %copy-start = (f32[8,4,1920]{2,1,0:T(4,128)S(1)}, f32[8,4,1920]{2,1,0:T(4,128)}, u32[]{:S(2)}) copy-start(f32[8,4,1920]{2,1,0:T(4,128)} %xv_ref.1) | copy-start | bytes 737284
